TPU v7x, 128 devices: a whole 4x4x4 slice. The times are simulated.
128 devices in a mesh: rows: 64 (over y, z, x), cols: 2 (over core).
Axes of the slice: x: 4, y: 4, z: 4, core: 2. Of those that a mesh axis runs over, the one named last changes fastest.
Arguments:
- video: bfloat16 [512, 256, 256], P('rows', 'cols'), may hold values from -12 to 12
- foreground: float32 [512, 256, 256], P('rows', 'cols'), may hold values from -4 to 4
- scaled_dual: float32 [512, 256, 256], P('rows', 'cols'), may hold values from -2.5 to 2.5
Outputs:
- background: float32 [512, 256, 256], P('rows', 'cols')
- new_foreground: float32 [512, 256, 256], P('rows', 'cols')
- new_dual: float32 [512, 256, 256], P('rows', 'cols')
All inputs are finite; a program needn't handle non-finite values.
Results may differ from a plain program's by a relative error of at most 0.00035.
Values sent between devices are 32-bit elements; how exact they have to be, the bound alone decides.
A program may use at most 64 MiB of HBM per device.

v0:
```python
import jax
import jax.numpy as jnp
from jax import lax
from jax.sharding import PartitionSpec as P

K_ROOT = 8
K_SIGN = 6
K_TV = 8
threshold_ratio = 1.0
dual_step = 0.25
tv_weight = 1.0


def shifted(x, axis, by):
    length = lax.axis_size(axis)
    pairs = [(i, i + by) for i in range(length) if 0 <= i + by < length]
    return lax.ppermute(x, axis, pairs)


def matmul(left, right):
    return jnp.dot(left, right, precision=lax.Precision.HIGHEST, preferred_element_type=jnp.float32)


def shrink_matrix(gram):
    size = gram.shape[0]
    identity = jnp.eye(size, dtype=jnp.float32)
    scale = jnp.sqrt(jnp.sum(gram * gram))
    root = gram / scale
    inverse = identity
    for sweep in range(K_ROOT):
        factor = 1.5 * identity - 0.5 * matmul(inverse, root)
        root = matmul(root, factor)
        inverse = matmul(factor, inverse)
    cutoff = threshold_ratio * jnp.trace(root) / size
    signed = root - cutoff * identity
    for sweep in range(K_SIGN):
        signed = 1.5 * signed - 0.5 * matmul(signed, matmul(signed, signed))
    return 0.5 * matmul(identity - cutoff * inverse, identity + signed)


def per_device(video, foreground, scaled_dual):
    rows_here, cols_here, frames = foreground.shape
    observed = video.astype(jnp.float32)
    mixed = observed - foreground + scaled_dual
    flat = mixed.reshape(-1, frames)
    gram = lax.psum(matmul(flat.T, flat), ("rows", "cols"))
    shrink = shrink_matrix(gram)
    background = matmul(flat, shrink).reshape(foreground.shape)
    target = observed - background + scaled_dual
    last_row = lax.axis_index("rows") == lax.axis_size("rows") - 1
    last_col = lax.axis_index("cols") == lax.axis_size("cols") - 1
    row_iota = lax.broadcasted_iota(jnp.int32, (rows_here, 1, 1), 0)
    col_iota = lax.broadcasted_iota(jnp.int32, (1, cols_here, 1), 1)
    row_keep = jnp.where(last_row & (row_iota == rows_here - 1), 0.0, 1.0).astype(jnp.float32)
    col_keep = jnp.where(last_col & (col_iota == cols_here - 1), 0.0, 1.0).astype(jnp.float32)
    dual_x = jnp.zeros_like(target)
    dual_y = jnp.zeros_like(target)

    def current_of(px, py):
        prev_x = shifted(px[-1:], "rows", 1)
        prev_y = shifted(py[:, -1:], "cols", 1)
        before_x = jnp.concatenate([prev_x, px[:-1]], axis=0)
        before_y = jnp.concatenate([prev_y, py[:, :-1]], axis=1)
        return target - (before_x - px + before_y - py)

    for sweep in range(K_TV):
        current = current_of(dual_x, dual_y)
        below = shifted(current[:1], "rows", -1)
        beside = shifted(current[:, :1], "cols", -1)
        down = (jnp.concatenate([current[1:], below], axis=0) - current) * row_keep
        across = (jnp.concatenate([current[:, 1:], beside], axis=1) - current) * col_keep
        dual_x = jnp.clip(dual_x + dual_step * down, -tv_weight, tv_weight)
        dual_y = jnp.clip(dual_y + dual_step * across, -tv_weight, tv_weight)
    new_foreground = current_of(dual_x, dual_y)
    new_dual = scaled_dual + observed - background - new_foreground
    return (background, new_foreground, new_dual)


def solution(mesh):
    return jax.shard_map(
        per_device,
        mesh=mesh,
        in_specs=(P("rows", "cols", None), P("rows", "cols", None), P("rows", "cols", None)),
        out_specs=(P("rows", "cols", None), P("rows", "cols", None), P("rows", "cols", None)),
        check_vma=False,
    )
```

profile of v0, /device:TPU:8, one launch (start us, length us, event | category | flops | bytes accessed | tf_op | source)
XLA Modules:
  0.0 340.7 jit_solution(16229040897291042421)
XLA Ops:
  7.2 5.1 %convolution_bitcast_fusion = f32[256,256]{1,0:T(8,128)} fusion(f32[8,128,256]{2,1,0:T(8,128)} %param.5, f32[8,128,256]{2,1,0:T(8,128)} %param.4, bf16[8,128,256]{2,1,0:T(8,128)(2,1)} %param.3), kind=kOutput, calls=%fused_computation.36 | convolution fusion | flops 806092800 | bytes 2883584 | tf_op jit(solution)/shard_map/dot_general | solution.py:21
  14.1 3.4 collective-permute-start
  17.5 140.5 %all-reduce.4.cloned.1.call-done = f32[256,256]{1,0:T(8,128)} async-done(((f32[256,256]{1,0:T(8,128)}), f32[256,256]{1,0:T(8,128)}) %all-reduce.4.cloned.1.call-update) | async-done | bytes 262160 | tf_op jit(solution)/shard_map/psum | solution.py:46
  178.9 5.3 %collective-permute-start.2 = (f32[1,128,256]{2,1,0:T(8,128)S(1)}, f32[1,128,256]{2,1,0:T(8,128)S(1)}, u32[]{:S(2)}, u32[]{:S(2)}) collective-permute-start(f32[1,128,256]{2,1,0:T(8,128)S(1)} %slice.267), channel_id=1, source_target_pairs={{2,0},{4,2},{6,4},{8,6},{10,8},{12,10},{14,12},{16,14},{18,16},{20... | collective-permute-start | bytes 393224 | tf_op jit(solution)/shard_map/ppermute | solution.py:17
  187.7 2.1 collective-permute-start.3
  192.6 6.8 %collective-permute-done.3 = f32[1,128,256]{2,1,0:T(8,128)S(1)} collective-permute-done((f32[1,128,256]{2,1,0:T(8,128)S(1)}, f32[1,128,256]{2,1,0:T(8,128)S(1)}, u32[]{:S(2)}, u32[]{:S(2)}) %collective-permute-start.3) | collective-permute-done | bytes 131104 | tf_op jit(solution)/shard_map/ppermute | solution.py:17
  199.8 3.5 %collective-permute-start.6 = (f32[1,128,256]{2,1,0:T(8,128)S(1)}, f32[1,128,256]{2,1,0:T(8,128)S(1)}, u32[]{:S(2)}, u32[]{:S(2)}) collective-permute-start(f32[1,128,256]{2,1,0:T(8,128)S(1)} %slice.275), channel_id=1, source_target_pairs={{2,0},{4,2},{6,4},{8,6},{10,8},{12,10},{14,12},{16,14},{18,16},{20... | collective-permute-start | bytes 393224 | tf_op jit(solution)/shard_map/ppermute | solution.py:17
  207.2 2.1 collective-permute-start.7
  211.9 6.7 %collective-permute-done.7 = f32[1,128,256]{2,1,0:T(8,128)S(1)} collective-permute-done((f32[1,128,256]{2,1,0:T(8,128)S(1)}, f32[1,128,256]{2,1,0:T(8,128)S(1)}, u32[]{:S(2)}, u32[]{:S(2)}) %collective-permute-start.7) | collective-permute-done | bytes 131104 | tf_op jit(solution)/shard_map/ppermute | solution.py:17
  219.0 3.2 collective-permute-start.10
  226.4 2.1 collective-permute-start.11
  231.1 6.4 %collective-permute-done.11 = f32[1,128,256]{2,1,0:T(8,128)S(1)} collective-permute-done((f32[1,128,256]{2,1,0:T(8,128)S(1)}, f32[1,128,256]{2,1,0:T(8,128)S(1)}, u32[]{:S(2)}, u32[]{:S(2)}) %collective-permute-start.11) | collective-permute-done | bytes 131104 | tf_op jit(solution)/shard_map/ppermute | solution.py:17
  237.9 3.2 collective-permute-start.14
  250.0 6.4 %collective-permute-done.15 = f32[1,128,256]{2,1,0:T(8,128)S(1)} collective-permute-done((f32[1,128,256]{2,1,0:T(8,128)S(1)}, f32[1,128,256]{2,1,0:T(8,128)S(1)}, u32[]{:S(2)}, u32[]{:S(2)}) %collective-permute-start.15) | collective-permute-done | bytes 131104 | tf_op jit(solution)/shard_map/ppermute | solution.py:17
  256.7 3.2 collective-permute-start.18
  268.8 6.4 %collective-permute-done.19 = f32[1,128,256]{2,1,0:T(8,128)S(1)} collective-permute-done((f32[1,128,256]{2,1,0:T(8,128)S(1)}, f32[1,128,256]{2,1,0:T(8,128)S(1)}, u32[]{:S(2)}, u32[]{:S(2)}) %collective-permute-start.19) | collective-permute-done | bytes 131104 | tf_op jit(solution)/shard_map/ppermute | solution.py:17
  275.6 3.2 collective-permute-start.22
  287.7 6.4 %collective-permute-done.23 = f32[1,128,256]{2,1,0:T(8,128)S(1)} collective-permute-done((f32[1,128,256]{2,1,0:T(8,128)S(1)}, f32[1,128,256]{2,1,0:T(8,128)S(1)}, u32[]{:S(2)}, u32[]{:S(2)}) %collective-permute-start.23) | collective-permute-done | bytes 131104 | tf_op jit(solution)/shard_map/ppermute | solution.py:17
  294.4 3.2 collective-permute-start.26
  301.8 2.1 collective-permute-start.27
  306.5 6.4 %collective-permute-done.27 = f32[1,128,256]{2,1,0:T(8,128)S(1)} collective-permute-done((f32[1,128,256]{2,1,0:T(8,128)S(1)}, f32[1,128,256]{2,1,0:T(8,128)S(1)}, u32[]{:S(2)}, u32[]{:S(2)}) %collective-permute-start.27) | collective-permute-done | bytes 131104 | tf_op jit(solution)/shard_map/ppermute | solution.py:17
  313.3 3.2 collective-permute-start.30
  320.7 2.2 collective-permute-start.31
  325.7 6.2 %collective-permute-done.31 = f32[1,128,256]{2,1,0:T(8,128)S(1)} collective-permute-done((f32[1,128,256]{2,1,0:T(8,128)S(1)}, f32[1,128,256]{2,1,0:T(8,128)S(1)}, u32[]{:S(2)}, u32[]{:S(2)}) %collective-permute-start.31) | collective-permute-done | bytes 131104 | tf_op jit(solution)/shard_map/ppermute | solution.py:17
  (175 shorter events, 85.1 us)
Async XLA Ops:
  7.2 150.9 %all-reduce.4.cloned.1.call-start = ((), (), s32[]{:S(2)}) async-start(), calls=%async_computation | async-start | bytes 524288 | tf_op jit(solution)/shard_map/psum | solution.py:46
  12.4 163.8 %collective-permute-start.1 = (f32[8,1,256]{2,1,0:T(1,128)S(1)}, f32[8,1,256]{2,1,0:T(1,128)S(1)}, u32[]{:S(2)}, u32[]{:S(2)}) collective-permute-start(f32[8,1,256]{2,1,0:T(1,128)S(1)} %slice.201), channel_id=1, source_target_pairs={{0,1},{2,3},{4,5},{6,7},{8,9},{10,11},{12,13},{14,15},{16,17},{18,... | collective-permute-start | bytes 24584 | tf_op jit(solution)/shard_map/ppermute | solution.py:17
  14.1 162.0 %collective-permute-start = (f32[1,128,256]{2,1,0:T(8,128)S(1)}, f32[1,128,256]{2,1,0:T(8,128)S(1)}, u32[]{:S(2)}, u32[]{:S(2)}) collective-permute-start(f32[1,128,256]{2,1,0:T(8,128)S(1)} %slice.200), channel_id=1, source_target_pairs={{0,2},{2,4},{4,6},{6,8},{8,10},{10,12},{12,14},{14,16},{16,18},{18... | collective-permute-start | bytes 393224 | tf_op jit(solution)/shard_map/ppermute | solution.py:17
  178.9 8.4 %collective-permute-start.2 = (f32[1,128,256]{2,1,0:T(8,128)S(1)}, f32[1,128,256]{2,1,0:T(8,128)S(1)}, u32[]{:S(2)}, u32[]{:S(2)}) collective-permute-start(f32[1,128,256]{2,1,0:T(8,128)S(1)} %slice.267), channel_id=1, source_target_pairs={{2,0},{4,2},{6,4},{8,6},{10,8},{12,10},{14,12},{16,14},{18,16},{20... | collective-permute-start | bytes 393224 | tf_op jit(solution)/shard_map/ppermute | solution.py:17
  187.7 11.7 %collective-permute-start.3 = (f32[1,128,256]{2,1,0:T(8,128)S(1)}, f32[1,128,256]{2,1,0:T(8,128)S(1)}, u32[]{:S(2)}, u32[]{:S(2)}) collective-permute-start(f32[1,128,256]{2,1,0:T(8,128)S(1)} %slice.268), channel_id=1, source_target_pairs={{0,2},{2,4},{4,6},{6,8},{8,10},{10,12},{12,14},{14,16},{16,18},{18... | collective-permute-start | bytes 393224 | tf_op jit(solution)/shard_map/ppermute | solution.py:17
  199.8 6.9 %collective-permute-start.6 = (f32[1,128,256]{2,1,0:T(8,128)S(1)}, f32[1,128,256]{2,1,0:T(8,128)S(1)}, u32[]{:S(2)}, u32[]{:S(2)}) collective-permute-start(f32[1,128,256]{2,1,0:T(8,128)S(1)} %slice.275), channel_id=1, source_target_pairs={{2,0},{4,2},{6,4},{8,6},{10,8},{12,10},{14,12},{16,14},{18,16},{20... | collective-permute-start | bytes 393224 | tf_op jit(solution)/shard_map/ppermute | solution.py:17
  203.4 3.1 collective-permute-start.8
  207.2 11.5 %collective-permute-start.7 = (f32[1,128,256]{2,1,0:T(8,128)S(1)}, f32[1,128,256]{2,1,0:T(8,128)S(1)}, u32[]{:S(2)}, u32[]{:S(2)}) collective-permute-start(f32[1,128,256]{2,1,0:T(8,128)S(1)} %slice.276), channel_id=1, source_target_pairs={{0,2},{2,4},{4,6},{6,8},{8,10},{10,12},{12,14},{14,16},{16,18},{18... | collective-permute-start | bytes 393224 | tf_op jit(solution)/shard_map/ppermute | solution.py:17
  219.0 6.9 %collective-permute-start.10 = (f32[1,128,256]{2,1,0:T(8,128)S(1)}, f32[1,128,256]{2,1,0:T(8,128)S(1)}, u32[]{:S(2)}, u32[]{:S(2)}) collective-permute-start(f32[1,128,256]{2,1,0:T(8,128)S(1)} %slice.283), channel_id=1, source_target_pairs={{2,0},{4,2},{6,4},{8,6},{10,8},{12,10},{14,12},{16,14},{18,16},{20... | collective-permute-start | bytes 393224 | tf_op jit(solution)/shard_map/ppermute | solution.py:17
  226.4 11.1 %collective-permute-start.11 = (f32[1,128,256]{2,1,0:T(8,128)S(1)}, f32[1,128,256]{2,1,0:T(8,128)S(1)}, u32[]{:S(2)}, u32[]{:S(2)}) collective-permute-start(f32[1,128,256]{2,1,0:T(8,128)S(1)} %slice.284), channel_id=1, source_target_pairs={{0,2},{2,4},{4,6},{6,8},{8,10},{10,12},{12,14},{14,16},{16,18},{18... | collective-permute-start | bytes 393224 | tf_op jit(solution)/shard_map/ppermute | solution.py:17
  237.9 6.9 %collective-permute-start.14 = (f32[1,128,256]{2,1,0:T(8,128)S(1)}, f32[1,128,256]{2,1,0:T(8,128)S(1)}, u32[]{:S(2)}, u32[]{:S(2)}) collective-permute-start(f32[1,128,256]{2,1,0:T(8,128)S(1)} %slice.291), channel_id=1, source_target_pairs={{2,0},{4,2},{6,4},{8,6},{10,8},{12,10},{14,12},{16,14},{18,16},{20... | collective-permute-start | bytes 393224 | tf_op jit(solution)/shard_map/ppermute | solution.py:17
  241.1 3.1 collective-permute-start.16
  245.3 11.1 %collective-permute-start.15 = (f32[1,128,256]{2,1,0:T(8,128)S(1)}, f32[1,128,256]{2,1,0:T(8,128)S(1)}, u32[]{:S(2)}, u32[]{:S(2)}) collective-permute-start(f32[1,128,256]{2,1,0:T(8,128)S(1)} %slice.292), channel_id=1, source_target_pairs={{0,2},{2,4},{4,6},{6,8},{8,10},{10,12},{12,14},{14,16},{16,18},{18... | collective-permute-start | bytes 393224 | tf_op jit(solution)/shard_map/ppermute | solution.py:17
  256.7 6.9 %collective-permute-start.18 = (f32[1,128,256]{2,1,0:T(8,128)S(1)}, f32[1,128,256]{2,1,0:T(8,128)S(1)}, u32[]{:S(2)}, u32[]{:S(2)}) collective-permute-start(f32[1,128,256]{2,1,0:T(8,128)S(1)} %slice.299), channel_id=1, source_target_pairs={{2,0},{4,2},{6,4},{8,6},{10,8},{12,10},{14,12},{16,14},{18,16},{20... | collective-permute-start | bytes 393224 | tf_op jit(solution)/shard_map/ppermute | solution.py:17
  259.9 3.1 collective-permute-start.20
  264.1 11.1 %collective-permute-start.19 = (f32[1,128,256]{2,1,0:T(8,128)S(1)}, f32[1,128,256]{2,1,0:T(8,128)S(1)}, u32[]{:S(2)}, u32[]{:S(2)}) collective-permute-start(f32[1,128,256]{2,1,0:T(8,128)S(1)} %slice.300), channel_id=1, source_target_pairs={{0,2},{2,4},{4,6},{6,8},{8,10},{10,12},{12,14},{14,16},{16,18},{18... | collective-permute-start | bytes 393224 | tf_op jit(solution)/shard_map/ppermute | solution.py:17
  275.6 6.9 %collective-permute-start.22 = (f32[1,128,256]{2,1,0:T(8,128)S(1)}, f32[1,128,256]{2,1,0:T(8,128)S(1)}, u32[]{:S(2)}, u32[]{:S(2)}) collective-permute-start(f32[1,128,256]{2,1,0:T(8,128)S(1)} %slice.307), channel_id=1, source_target_pairs={{2,0},{4,2},{6,4},{8,6},{10,8},{12,10},{14,12},{16,14},{18,16},{20... | collective-permute-start | bytes 393224 | tf_op jit(solution)/shard_map/ppermute | solution.py:17
  278.8 3.1 collective-permute-start.24
  283.0 11.1 %collective-permute-start.23 = (f32[1,128,256]{2,1,0:T(8,128)S(1)}, f32[1,128,256]{2,1,0:T(8,128)S(1)}, u32[]{:S(2)}, u32[]{:S(2)}) collective-permute-start(f32[1,128,256]{2,1,0:T(8,128)S(1)} %slice.308), channel_id=1, source_target_pairs={{0,2},{2,4},{4,6},{6,8},{8,10},{10,12},{12,14},{14,16},{16,18},{18... | collective-permute-start | bytes 393224 | tf_op jit(solution)/shard_map/ppermute | solution.py:17
  294.4 6.9 %collective-permute-start.26 = (f32[1,128,256]{2,1,0:T(8,128)S(1)}, f32[1,128,256]{2,1,0:T(8,128)S(1)}, u32[]{:S(2)}, u32[]{:S(2)}) collective-permute-start(f32[1,128,256]{2,1,0:T(8,128)S(1)} %slice.315), channel_id=1, source_target_pairs={{2,0},{4,2},{6,4},{8,6},{10,8},{12,10},{14,12},{16,14},{18,16},{20... | collective-permute-start | bytes 393224 | tf_op jit(solution)/shard_map/ppermute | solution.py:17
  297.6 3.1 collective-permute-start.28
  301.8 11.1 %collective-permute-start.27 = (f32[1,128,256]{2,1,0:T(8,128)S(1)}, f32[1,128,256]{2,1,0:T(8,128)S(1)}, u32[]{:S(2)}, u32[]{:S(2)}) collective-permute-start(f32[1,128,256]{2,1,0:T(8,128)S(1)} %slice.316), channel_id=1, source_target_pairs={{0,2},{2,4},{4,6},{6,8},{8,10},{10,12},{12,14},{14,16},{16,18},{18... | collective-permute-start | bytes 393224 | tf_op jit(solution)/shard_map/ppermute | solution.py:17
  313.3 6.9 %collective-permute-start.30 = (f32[1,128,256]{2,1,0:T(8,128)S(1)}, f32[1,128,256]{2,1,0:T(8,128)S(1)}, u32[]{:S(2)}, u32[]{:S(2)}) collective-permute-start(f32[1,128,256]{2,1,0:T(8,128)S(1)} %slice.323), channel_id=1, source_target_pairs={{2,0},{4,2},{6,4},{8,6},{10,8},{12,10},{14,12},{16,14},{18,16},{20... | collective-permute-start | bytes 393224 | tf_op jit(solution)/shard_map/ppermute | solution.py:17
  320.7 11.2 %collective-permute-start.31 = (f32[1,128,256]{2,1,0:T(8,128)S(1)}, f32[1,128,256]{2,1,0:T(8,128)S(1)}, u32[]{:S(2)}, u32[]{:S(2)}) collective-permute-start(f32[1,128,256]{2,1,0:T(8,128)S(1)} %slice.324), channel_id=1, source_target_pairs={{0,2},{2,4},{4,6},{6,8},{8,10},{10,12},{12,14},{14,16},{16,18},{18... | collective-permute-start | bytes 393224 | tf_op jit(solution)/shard_map/ppermute | solution.py:17
  (17 other events, 57.2 us)
Sparse Core Ops, SparseCore 0:
  13.3 144.7 all-reduce.3
where the time goes:
time: 342 us; the launch traced here: 341 us
  waiting for transfers between devices  214 us (63%)
  starting transfers between devices  74.6 us (22%)
  matrix products  21.9 us (6%)
  between operations  16.6 us (5%)
  other arithmetic  10.1 us (3%)
    psum x1, waiting for transfers between devices, per_device(): gram = lax.psum(matmul(flat.T, flat), ('rows', 'cols'))  141 us
    ppermute x34, starting transfers between devices, shifted(): return lax.ppermute(x, axis, pairs)  74.6 us
    ppermute x34, waiting for transfers between devices, shifted(): return lax.ppermute(x, axis, pairs)  74 us
    dot_general x39, matrix products, matmul(): jnp.dot(left, right, precision=lax.Precision.HIGHEST, preferred_element_t...  21.9 us
  transfers between devices with their start and end apart: 35, of which 32 were waited for; matrix products, arithmetic and copies ran while one was open for 5% of the time, Pallas kernels for 0%

commit v1 on v0

--- a/solution.py
+++ b/solution.py
@@ -43,7 +43,9 @@
     observed = video.astype(jnp.float32)
     mixed = observed - foreground + scaled_dual
     flat = mixed.reshape(-1, frames)
-    gram = lax.psum(matmul(flat.T, flat), ("rows", "cols"))
+    part = matmul(flat.T, flat)
+    blocks = lax.all_gather(part, ("rows", "cols"), axis=0, tiled=False)
+    gram = blocks.sum(axis=0)
     shrink = shrink_matrix(gram)
     background = matmul(flat, shrink).reshape(foreground.shape)
     target = observed - background + scaled_dual

time: 342 us -> 317 us (0.927)
  waiting for transfers between devices: 214 us -> 178 us
  other arithmetic: 10.1 us -> 21.5 us
    psum x1 -> x0, waiting for transfers between devices: 141 us -> none  [per_device(): gram = lax.psum(matmul(flat.T, flat), ('rows', 'cols'))]
    all_gather x0 -> x1, waiting for transfers between devices: none -> 104 us  [per_device(): blocks = lax.all_gather(part, ('rows', 'cols'), axis=0, tiled=False)]
    reduce_sum x0 -> x1, other arithmetic: none -> 12.1 us  [per_device(): gram = blocks.sum(axis=0)]
  transfers between devices with their start and end apart: 35 -> 35, of which waited for: 32 -> 32; matrix products, arithmetic and copies ran while one was open for 5% -> 9% of each run, Pallas kernels for 0% -> 0%
where the time goes in v1:
time: 317 us; the launch traced here: 316 us
  waiting for transfers between devices  178 us (56%)
  starting transfers between devices  74.4 us (23%)
  matrix products  23.5 us (7%)
  other arithmetic  21.5 us (7%)
  between operations  16.5 us (5%)
    all_gather x1, waiting for transfers between devices, per_device(): blocks = lax.all_gather(part, ('rows', 'cols'), axis=0, tiled=False)  104 us
    ppermute x34, starting transfers between devices, shifted(): return lax.ppermute(x, axis, pairs)  74.4 us
    ppermute x34, waiting for transfers between devices, shifted(): return lax.ppermute(x, axis, pairs)  74.1 us
    dot_general x39, matrix products, matmul(): jnp.dot(left, right, precision=lax.Precision.HIGHEST, preferred_element_t...  23.5 us
    reduce_sum x1, other arithmetic, per_device(): gram = blocks.sum(axis=0)  12.1 us
  transfers between devices with their start and end apart: 35, of which 32 were waited for; matrix products, arithmetic and copies ran while one was open for 9% of the time, Pallas kernels for 0%

profile of v1, /device:TPU:8, one launch (start us, length us, event | category | flops | bytes accessed | tf_op | source)
XLA Modules:
  0.0 316.3 jit_solution(13586562370315680722)
XLA Ops:
  7.2 5.2 %convolution_bitcast_fusion = f32[256,256]{1,0:T(8,128)} fusion(f32[8,128,256]{2,1,0:T(8,128)} %param.5, f32[8,128,256]{2,1,0:T(8,128)} %param.4, bf16[8,128,256]{2,1,0:T(8,128)(2,1)} %param.3), kind=kOutput, calls=%fused_computation.36 | convolution fusion | flops 806092800 | bytes 2883584 | tf_op jit(solution)/shard_map/dot_general | solution.py:21
  12.5 3.4 %collective-permute-start = (f32[1,128,256]{2,1,0:T(8,128)S(1)}, f32[1,128,256]{2,1,0:T(8,128)S(1)}, u32[]{:S(2)}, u32[]{:S(2)}) collective-permute-start(f32[1,128,256]{2,1,0:T(8,128)S(1)} %slice.200), channel_id=1, source_target_pairs={{0,2},{2,4},{4,6},{6,8},{8,10},{10,12},{12,14},{14,16},{16,18},{18... | collective-permute-start | bytes 393224 | tf_op jit(solution)/shard_map/ppermute | solution.py:17
  17.4 103.8 %all-gather.3.cloned.1.call-done = f32[32768,256]{1,0:T(8,128)} async-done(((f32[256,256]{1,0:T(8,128)}), f32[32768,256]{1,0:T(8,128)}) %all-gather.3.cloned.1.call-update) | async-done | bytes 33554448 | tf_op jit(solution)/shard_map/all_gather | solution.py:47
  121.2 12.1 %reduce_sum.28 = f32[256,256]{1,0:T(8,128)S(1)} reduce(f32[128,256,256]{2,1,0:T(8,128)} %bitcast.81, f32[]{:T(128)} %constant.13.clone.1), dimensions={0}, to_apply=%region_0.0 | reduce | flops 8323072 | bytes 33816580 | tf_op jit(solution)/shard_map/reduce_sum | solution.py:48
  150.5 3.5 %add_subtract_fusion = (f32[8,128,256]{2,1,0:T(8,128)S(1)}, f32[8,128,256]{2,1,0:T(8,128)S(1)}, f32[8,128,256]{2,1,0:T(8,128)}) fusion(f32[8,1,256]{2,1,0:T(1,128)S(1)} %collective-permute-done.1, f32[1,128,256]{2,1,0:T(8,128)S(1)} %collective-permute-done, f32[8,128,256]{2,1,0:T(8,128)S(1)} %copy-done, bf16[8,128,256]{2,1,0:T(8,128)(2,1)} %param.3, ...), kind=kOutput, calls=%fused_computation.151 | convolution fusion | flops 807403520 | bytes 6168576 | tf_op jit(solution)/shard_map/dot_general | solution.py:21
  154.0 5.3 %collective-permute-start.2 = (f32[1,128,256]{2,1,0:T(8,128)S(1)}, f32[1,128,256]{2,1,0:T(8,128)S(1)}, u32[]{:S(2)}, u32[]{:S(2)}) collective-permute-start(f32[1,128,256]{2,1,0:T(8,128)S(1)} %slice.267), channel_id=1, source_target_pairs={{2,0},{4,2},{6,4},{8,6},{10,8},{12,10},{14,12},{16,14},{18,16},{20... | collective-permute-start | bytes 393224 | tf_op jit(solution)/shard_map/ppermute | solution.py:17
  163.0 2.5 collective-permute-start.3
  167.7 6.9 %collective-permute-done.3 = f32[1,128,256]{2,1,0:T(8,128)S(1)} collective-permute-done((f32[1,128,256]{2,1,0:T(8,128)S(1)}, f32[1,128,256]{2,1,0:T(8,128)S(1)}, u32[]{:S(2)}, u32[]{:S(2)}) %collective-permute-start.3) | collective-permute-done | bytes 131104 | tf_op jit(solution)/shard_map/ppermute | solution.py:17
  175.0 3.8 %collective-permute-start.6 = (f32[1,128,256]{2,1,0:T(8,128)S(1)}, f32[1,128,256]{2,1,0:T(8,128)S(1)}, u32[]{:S(2)}, u32[]{:S(2)}) collective-permute-start(f32[1,128,256]{2,1,0:T(8,128)S(1)} %slice.275), channel_id=1, source_target_pairs={{2,0},{4,2},{6,4},{8,6},{10,8},{12,10},{14,12},{16,14},{18,16},{20... | collective-permute-start | bytes 393224 | tf_op jit(solution)/shard_map/ppermute | solution.py:17
  187.3 6.8 %collective-permute-done.7 = f32[1,128,256]{2,1,0:T(8,128)S(1)} collective-permute-done((f32[1,128,256]{2,1,0:T(8,128)S(1)}, f32[1,128,256]{2,1,0:T(8,128)S(1)}, u32[]{:S(2)}, u32[]{:S(2)}) %collective-permute-start.7) | collective-permute-done | bytes 131104 | tf_op jit(solution)/shard_map/ppermute | solution.py:17
  194.5 3.2 %collective-permute-start.10 = (f32[1,128,256]{2,1,0:T(8,128)S(1)}, f32[1,128,256]{2,1,0:T(8,128)S(1)}, u32[]{:S(2)}, u32[]{:S(2)}) collective-permute-start(f32[1,128,256]{2,1,0:T(8,128)S(1)} %slice.283), channel_id=1, source_target_pairs={{2,0},{4,2},{6,4},{8,6},{10,8},{12,10},{14,12},{16,14},{18,16},{20... | collective-permute-start | bytes 393224 | tf_op jit(solution)/shard_map/ppermute | solution.py:17
  206.6 6.4 %collective-permute-done.11 = f32[1,128,256]{2,1,0:T(8,128)S(1)} collective-permute-done((f32[1,128,256]{2,1,0:T(8,128)S(1)}, f32[1,128,256]{2,1,0:T(8,128)S(1)}, u32[]{:S(2)}, u32[]{:S(2)}) %collective-permute-start.11) | collective-permute-done | bytes 131104 | tf_op jit(solution)/shard_map/ppermute | solution.py:17
  213.3 3.2 %collective-permute-start.14 = (f32[1,128,256]{2,1,0:T(8,128)S(1)}, f32[1,128,256]{2,1,0:T(8,128)S(1)}, u32[]{:S(2)}, u32[]{:S(2)}) collective-permute-start(f32[1,128,256]{2,1,0:T(8,128)S(1)} %slice.291), channel_id=1, source_target_pairs={{2,0},{4,2},{6,4},{8,6},{10,8},{12,10},{14,12},{16,14},{18,16},{20... | collective-permute-start | bytes 393224 | tf_op jit(solution)/shard_map/ppermute | solution.py:17
  225.4 6.4 %collective-permute-done.15 = f32[1,128,256]{2,1,0:T(8,128)S(1)} collective-permute-done((f32[1,128,256]{2,1,0:T(8,128)S(1)}, f32[1,128,256]{2,1,0:T(8,128)S(1)}, u32[]{:S(2)}, u32[]{:S(2)}) %collective-permute-start.15) | collective-permute-done | bytes 131104 | tf_op jit(solution)/shard_map/ppermute | solution.py:17
  232.2 3.2 %collective-permute-start.18 = (f32[1,128,256]{2,1,0:T(8,128)S(1)}, f32[1,128,256]{2,1,0:T(8,128)S(1)}, u32[]{:S(2)}, u32[]{:S(2)}) collective-permute-start(f32[1,128,256]{2,1,0:T(8,128)S(1)} %slice.299), channel_id=1, source_target_pairs={{2,0},{4,2},{6,4},{8,6},{10,8},{12,10},{14,12},{16,14},{18,16},{20... | collective-permute-start | bytes 393224 | tf_op jit(solution)/shard_map/ppermute | solution.py:17
  244.4 6.4 %collective-permute-done.19 = f32[1,128,256]{2,1,0:T(8,128)S(1)} collective-permute-done((f32[1,128,256]{2,1,0:T(8,128)S(1)}, f32[1,128,256]{2,1,0:T(8,128)S(1)}, u32[]{:S(2)}, u32[]{:S(2)}) %collective-permute-start.19) | collective-permute-done | bytes 131104 | tf_op jit(solution)/shard_map/ppermute | solution.py:17
  251.1 3.2 %collective-permute-start.22 = (f32[1,128,256]{2,1,0:T(8,128)S(1)}, f32[1,128,256]{2,1,0:T(8,128)S(1)}, u32[]{:S(2)}, u32[]{:S(2)}) collective-permute-start(f32[1,128,256]{2,1,0:T(8,128)S(1)} %slice.307), channel_id=1, source_target_pairs={{2,0},{4,2},{6,4},{8,6},{10,8},{12,10},{14,12},{16,14},{18,16},{20... | collective-permute-start | bytes 393224 | tf_op jit(solution)/shard_map/ppermute | solution.py:17
  258.6 2.1 collective-permute-start.23
  263.3 6.4 %collective-permute-done.23 = f32[1,128,256]{2,1,0:T(8,128)S(1)} collective-permute-done((f32[1,128,256]{2,1,0:T(8,128)S(1)}, f32[1,128,256]{2,1,0:T(8,128)S(1)}, u32[]{:S(2)}, u32[]{:S(2)}) %collective-permute-start.23) | collective-permute-done | bytes 131104 | tf_op jit(solution)/shard_map/ppermute | solution.py:17
  270.1 3.2 %collective-permute-start.26 = (f32[1,128,256]{2,1,0:T(8,128)S(1)}, f32[1,128,256]{2,1,0:T(8,128)S(1)}, u32[]{:S(2)}, u32[]{:S(2)}) collective-permute-start(f32[1,128,256]{2,1,0:T(8,128)S(1)} %slice.315), channel_id=1, source_target_pairs={{2,0},{4,2},{6,4},{8,6},{10,8},{12,10},{14,12},{16,14},{18,16},{20... | collective-permute-start | bytes 393224 | tf_op jit(solution)/shard_map/ppermute | solution.py:17
  277.5 2.1 collective-permute-start.27
  282.3 6.4 %collective-permute-done.27 = f32[1,128,256]{2,1,0:T(8,128)S(1)} collective-permute-done((f32[1,128,256]{2,1,0:T(8,128)S(1)}, f32[1,128,256]{2,1,0:T(8,128)S(1)}, u32[]{:S(2)}, u32[]{:S(2)}) %collective-permute-start.27) | collective-permute-done | bytes 131104 | tf_op jit(solution)/shard_map/ppermute | solution.py:17
  289.0 3.2 %collective-permute-start.30 = (f32[1,128,256]{2,1,0:T(8,128)S(1)}, f32[1,128,256]{2,1,0:T(8,128)S(1)}, u32[]{:S(2)}, u32[]{:S(2)}) collective-permute-start(f32[1,128,256]{2,1,0:T(8,128)S(1)} %slice.323), channel_id=1, source_target_pairs={{2,0},{4,2},{6,4},{8,6},{10,8},{12,10},{14,12},{16,14},{18,16},{20... | collective-permute-start | bytes 393224 | tf_op jit(solution)/shard_map/ppermute | solution.py:17
  301.1 6.4 %collective-permute-done.31 = f32[1,128,256]{2,1,0:T(8,128)S(1)} collective-permute-done((f32[1,128,256]{2,1,0:T(8,128)S(1)}, f32[1,128,256]{2,1,0:T(8,128)S(1)}, u32[]{:S(2)}, u32[]{:S(2)}) %collective-permute-start.31) | collective-permute-done | bytes 131104 | tf_op jit(solution)/shard_map/ppermute | solution.py:17
  (170 shorter events, 84.9 us)
Async XLA Ops:
  7.2 114.1 %all-gather.3.cloned.1.call-start = ((), (), s32[]{:S(2)}) async-start(), calls=%async_computation | async-start | bytes 33816576 | tf_op jit(solution)/shard_map/all_gather | solution.py:47
  12.5 138.0 %collective-permute-start = (f32[1,128,256]{2,1,0:T(8,128)S(1)}, f32[1,128,256]{2,1,0:T(8,128)S(1)}, u32[]{:S(2)}, u32[]{:S(2)}) collective-permute-start(f32[1,128,256]{2,1,0:T(8,128)S(1)} %slice.200), channel_id=1, source_target_pairs={{0,2},{2,4},{4,6},{6,8},{8,10},{10,12},{12,14},{14,16},{16,18},{18... | collective-permute-start | bytes 393224 | tf_op jit(solution)/shard_map/ppermute | solution.py:17
  15.9 134.6 %collective-permute-start.1 = (f32[8,1,256]{2,1,0:T(1,128)S(1)}, f32[8,1,256]{2,1,0:T(1,128)S(1)}, u32[]{:S(2)}, u32[]{:S(2)}) collective-permute-start(f32[8,1,256]{2,1,0:T(1,128)S(1)} %slice.201), channel_id=1, source_target_pairs={{0,1},{2,3},{4,5},{6,7},{8,9},{10,11},{12,13},{14,15},{16,17},{18,... | collective-permute-start | bytes 24584 | tf_op jit(solution)/shard_map/ppermute | solution.py:17
  154.0 8.5 %collective-permute-start.2 = (f32[1,128,256]{2,1,0:T(8,128)S(1)}, f32[1,128,256]{2,1,0:T(8,128)S(1)}, u32[]{:S(2)}, u32[]{:S(2)}) collective-permute-start(f32[1,128,256]{2,1,0:T(8,128)S(1)} %slice.267), channel_id=1, source_target_pairs={{2,0},{4,2},{6,4},{8,6},{10,8},{12,10},{14,12},{16,14},{18,16},{20... | collective-permute-start | bytes 393224 | tf_op jit(solution)/shard_map/ppermute | solution.py:17
  163.0 11.7 %collective-permute-start.3 = (f32[1,128,256]{2,1,0:T(8,128)S(1)}, f32[1,128,256]{2,1,0:T(8,128)S(1)}, u32[]{:S(2)}, u32[]{:S(2)}) collective-permute-start(f32[1,128,256]{2,1,0:T(8,128)S(1)} %slice.268), channel_id=1, source_target_pairs={{0,2},{2,4},{4,6},{6,8},{8,10},{10,12},{12,14},{14,16},{16,18},{18... | collective-permute-start | bytes 393224 | tf_op jit(solution)/shard_map/ppermute | solution.py:17
  175.0 6.9 %collective-permute-start.6 = (f32[1,128,256]{2,1,0:T(8,128)S(1)}, f32[1,128,256]{2,1,0:T(8,128)S(1)}, u32[]{:S(2)}, u32[]{:S(2)}) collective-permute-start(f32[1,128,256]{2,1,0:T(8,128)S(1)} %slice.275), channel_id=1, source_target_pairs={{2,0},{4,2},{6,4},{8,6},{10,8},{12,10},{14,12},{16,14},{18,16},{20... | collective-permute-start | bytes 393224 | tf_op jit(solution)/shard_map/ppermute | solution.py:17
  182.4 11.7 %collective-permute-start.7 = (f32[1,128,256]{2,1,0:T(8,128)S(1)}, f32[1,128,256]{2,1,0:T(8,128)S(1)}, u32[]{:S(2)}, u32[]{:S(2)}) collective-permute-start(f32[1,128,256]{2,1,0:T(8,128)S(1)} %slice.276), channel_id=1, source_target_pairs={{0,2},{2,4},{4,6},{6,8},{8,10},{10,12},{12,14},{14,16},{16,18},{18... | collective-permute-start | bytes 393224 | tf_op jit(solution)/shard_map/ppermute | solution.py:17
  194.5 6.9 %collective-permute-start.10 = (f32[1,128,256]{2,1,0:T(8,128)S(1)}, f32[1,128,256]{2,1,0:T(8,128)S(1)}, u32[]{:S(2)}, u32[]{:S(2)}) collective-permute-start(f32[1,128,256]{2,1,0:T(8,128)S(1)} %slice.283), channel_id=1, source_target_pairs={{2,0},{4,2},{6,4},{8,6},{10,8},{12,10},{14,12},{16,14},{18,16},{20... | collective-permute-start | bytes 393224 | tf_op jit(solution)/shard_map/ppermute | solution.py:17
  197.7 3.1 collective-permute-start.12
  201.9 11.1 %collective-permute-start.11 = (f32[1,128,256]{2,1,0:T(8,128)S(1)}, f32[1,128,256]{2,1,0:T(8,128)S(1)}, u32[]{:S(2)}, u32[]{:S(2)}) collective-permute-start(f32[1,128,256]{2,1,0:T(8,128)S(1)} %slice.284), channel_id=1, source_target_pairs={{0,2},{2,4},{4,6},{6,8},{8,10},{10,12},{12,14},{14,16},{16,18},{18... | collective-permute-start | bytes 393224 | tf_op jit(solution)/shard_map/ppermute | solution.py:17
  213.3 6.9 %collective-permute-start.14 = (f32[1,128,256]{2,1,0:T(8,128)S(1)}, f32[1,128,256]{2,1,0:T(8,128)S(1)}, u32[]{:S(2)}, u32[]{:S(2)}) collective-permute-start(f32[1,128,256]{2,1,0:T(8,128)S(1)} %slice.291), channel_id=1, source_target_pairs={{2,0},{4,2},{6,4},{8,6},{10,8},{12,10},{14,12},{16,14},{18,16},{20... | collective-permute-start | bytes 393224 | tf_op jit(solution)/shard_map/ppermute | solution.py:17
  216.5 3.1 collective-permute-start.16
  220.7 11.1 %collective-permute-start.15 = (f32[1,128,256]{2,1,0:T(8,128)S(1)}, f32[1,128,256]{2,1,0:T(8,128)S(1)}, u32[]{:S(2)}, u32[]{:S(2)}) collective-permute-start(f32[1,128,256]{2,1,0:T(8,128)S(1)} %slice.292), channel_id=1, source_target_pairs={{0,2},{2,4},{4,6},{6,8},{8,10},{10,12},{12,14},{14,16},{16,18},{18... | collective-permute-start | bytes 393224 | tf_op jit(solution)/shard_map/ppermute | solution.py:17
  232.2 6.9 %collective-permute-start.18 = (f32[1,128,256]{2,1,0:T(8,128)S(1)}, f32[1,128,256]{2,1,0:T(8,128)S(1)}, u32[]{:S(2)}, u32[]{:S(2)}) collective-permute-start(f32[1,128,256]{2,1,0:T(8,128)S(1)} %slice.299), channel_id=1, source_target_pairs={{2,0},{4,2},{6,4},{8,6},{10,8},{12,10},{14,12},{16,14},{18,16},{20... | collective-permute-start | bytes 393224 | tf_op jit(solution)/shard_map/ppermute | solution.py:17
  235.4 3.1 collective-permute-start.20
  239.7 11.1 %collective-permute-start.19 = (f32[1,128,256]{2,1,0:T(8,128)S(1)}, f32[1,128,256]{2,1,0:T(8,128)S(1)}, u32[]{:S(2)}, u32[]{:S(2)}) collective-permute-start(f32[1,128,256]{2,1,0:T(8,128)S(1)} %slice.300), channel_id=1, source_target_pairs={{0,2},{2,4},{4,6},{6,8},{8,10},{10,12},{12,14},{14,16},{16,18},{18... | collective-permute-start | bytes 393224 | tf_op jit(solution)/shard_map/ppermute | solution.py:17
  251.1 6.9 %collective-permute-start.22 = (f32[1,128,256]{2,1,0:T(8,128)S(1)}, f32[1,128,256]{2,1,0:T(8,128)S(1)}, u32[]{:S(2)}, u32[]{:S(2)}) collective-permute-start(f32[1,128,256]{2,1,0:T(8,128)S(1)} %slice.307), channel_id=1, source_target_pairs={{2,0},{4,2},{6,4},{8,6},{10,8},{12,10},{14,12},{16,14},{18,16},{20... | collective-permute-start | bytes 393224 | tf_op jit(solution)/shard_map/ppermute | solution.py:17
  258.6 11.1 %collective-permute-start.23 = (f32[1,128,256]{2,1,0:T(8,128)S(1)}, f32[1,128,256]{2,1,0:T(8,128)S(1)}, u32[]{:S(2)}, u32[]{:S(2)}) collective-permute-start(f32[1,128,256]{2,1,0:T(8,128)S(1)} %slice.308), channel_id=1, source_target_pairs={{0,2},{2,4},{4,6},{6,8},{8,10},{10,12},{12,14},{14,16},{16,18},{18... | collective-permute-start | bytes 393224 | tf_op jit(solution)/shard_map/ppermute | solution.py:17
  270.1 6.9 %collective-permute-start.26 = (f32[1,128,256]{2,1,0:T(8,128)S(1)}, f32[1,128,256]{2,1,0:T(8,128)S(1)}, u32[]{:S(2)}, u32[]{:S(2)}) collective-permute-start(f32[1,128,256]{2,1,0:T(8,128)S(1)} %slice.315), channel_id=1, source_target_pairs={{2,0},{4,2},{6,4},{8,6},{10,8},{12,10},{14,12},{16,14},{18,16},{20... | collective-permute-start | bytes 393224 | tf_op jit(solution)/shard_map/ppermute | solution.py:17
  273.3 3.1 collective-permute-start.28
  277.5 11.1 %collective-permute-start.27 = (f32[1,128,256]{2,1,0:T(8,128)S(1)}, f32[1,128,256]{2,1,0:T(8,128)S(1)}, u32[]{:S(2)}, u32[]{:S(2)}) collective-permute-start(f32[1,128,256]{2,1,0:T(8,128)S(1)} %slice.316), channel_id=1, source_target_pairs={{0,2},{2,4},{4,6},{6,8},{8,10},{10,12},{12,14},{14,16},{16,18},{18... | collective-permute-start | bytes 393224 | tf_op jit(solution)/shard_map/ppermute | solution.py:17
  289.0 6.9 %collective-permute-start.30 = (f32[1,128,256]{2,1,0:T(8,128)S(1)}, f32[1,128,256]{2,1,0:T(8,128)S(1)}, u32[]{:S(2)}, u32[]{:S(2)}) collective-permute-start(f32[1,128,256]{2,1,0:T(8,128)S(1)} %slice.323), channel_id=1, source_target_pairs={{2,0},{4,2},{6,4},{8,6},{10,8},{12,10},{14,12},{16,14},{18,16},{20... | collective-permute-start | bytes 393224 | tf_op jit(solution)/shard_map/ppermute | solution.py:17
  292.2 3.1 collective-permute-start.32
  296.4 11.1 %collective-permute-start.31 = (f32[1,128,256]{2,1,0:T(8,128)S(1)}, f32[1,128,256]{2,1,0:T(8,128)S(1)}, u32[]{:S(2)}, u32[]{:S(2)}) collective-permute-start(f32[1,128,256]{2,1,0:T(8,128)S(1)} %slice.324), channel_id=1, source_target_pairs={{0,2},{2,4},{4,6},{6,8},{8,10},{10,12},{12,14},{14,16},{16,18},{18... | collective-permute-start | bytes 393224 | tf_op jit(solution)/shard_map/ppermute | solution.py:17
  (14 other events, 314.5 us)
Sparse Core Ops, SparseCore 0:
  12.6 108.5 all-gather.2
